TPU v7x, 32 devices: a whole 2x2x4 slice. The times are simulated.
32 devices in a mesh: gx: 4 (over z), gy: 4 (over x, core), gz: 2 (over y).
Axes of the slice: x: 2, y: 2, z: 4, core: 2. Of those that a mesh axis runs over, the one named last changes fastest.
Arguments:
- activations: bfloat16 [1024, 8192], P('gy', 'gx'), may hold values from -0.5 to 0.5
- cotangent: bfloat16 [1024, 8192], P('gy', 'gx'), may hold values from -1.5 to 1.5
- gate_pre: bfloat16 [1024, 26624], P('gx', ('gy', 'gz')), may hold values from -6 to 6
- up_pre: bfloat16 [1024, 26624], P('gx', ('gy', 'gz')), may hold values from -6 to 6
- gate_weight: bfloat16 [8192, 26624], P('gx', ('gy', 'gz')), may hold values from -0.0625 to 0.0625
- up_weight: bfloat16 [8192, 26624], P('gx', ('gy', 'gz')), may hold values from -0.0625 to 0.0625
- down_weight: bfloat16 [26624, 8192], P(('gy', 'gz'), 'gx'), may hold values from -0.15625 to 0.15625
Outputs:
- input_grad: bfloat16 [1024, 8192], P('gy', 'gx')
- gate_grad: bfloat16 [8192, 26624], P('gx', ('gy', 'gz'))
- up_grad: bfloat16 [8192, 26624], P('gx', ('gy', 'gz'))
- down_grad: bfloat16 [26624, 8192], P(('gy', 'gz'), 'gx')
All inputs are finite; a program needn't handle non-finite values.
Results may differ from a plain program's by a relative error of at most 0.015.
Values may be sent and summed in bfloat16 or wider, within the bound.
A program may use at most 192 MiB of HBM per device.

v0:
```python
import jax
import jax.numpy as jnp
from jax import lax
from jax.sharding import PartitionSpec as P

over_rows = (((0,), (0,)), ((), ()))
over_cols = (((1,), (1,)), ((), ()))


def swiglu_grads(gate_in, up_in, grad_hidden):
    gate_val = gate_in.astype(jnp.float32)
    up_val = up_in.astype(jnp.float32)
    sigmoid = jax.nn.sigmoid(gate_val)
    hidden = (gate_val * sigmoid * up_val).astype(jnp.bfloat16)
    grad_gate = (grad_hidden * up_val * sigmoid * (1.0 + gate_val * (1.0 - sigmoid))).astype(
        jnp.bfloat16
    )
    grad_up = (grad_hidden * gate_val * sigmoid).astype(jnp.bfloat16)
    return (hidden, grad_gate, grad_up)


def input_terms(grad_gate, grad_up, gate_weight, up_weight):

    def compute(offset, amount):
        total = lax.dot_general(
            grad_gate, gate_weight, over_cols, preferred_element_type=jnp.float32
        )
        return total + lax.dot_general(
            grad_up, up_weight, over_cols, preferred_element_type=jnp.float32
        )

    return compute


def shards(activations, cotangent, gate_pre, up_pre, gate_weight, up_weight, down_weight):
    cotangent_all = lax.all_gather(cotangent, "gy", axis=0, tiled=True)
    gate_all, up_all = (
        lax.all_gather(gate_pre, "gx", axis=0, tiled=True),
        lax.all_gather(up_pre, "gx", axis=0, tiled=True),
    )
    local_sum = lax.dot_general(
        cotangent_all, down_weight, over_cols, preferred_element_type=jnp.float32
    )
    grad_hidden = lax.psum(local_sum, "gx")
    hidden, grad_gate, grad_up = swiglu_grads(gate_all, up_all, grad_hidden)
    down_grad = lax.dot_general(
        hidden, cotangent_all, over_rows, preferred_element_type=jnp.float32
    ).astype(jnp.bfloat16)
    segment = lax.all_gather(activations, "gy", axis=0, tiled=True)
    first = lax.dot_general(segment, grad_gate, over_rows, preferred_element_type=jnp.float32)
    second = lax.dot_general(segment, grad_up, over_rows, preferred_element_type=jnp.float32)
    row_count = activations.shape[0]
    terms = input_terms(grad_gate, grad_up, gate_weight, up_weight)
    share_rows = row_count // lax.axis_size("gz")
    input_share = lax.psum_scatter(
        terms(jnp.int32(0), lax.axis_size(("gy", "gz")) * share_rows),
        ("gy", "gz"),
        scatter_dimension=0,
        tiled=True,
    )
    input_grad = lax.all_gather(input_share.astype(jnp.bfloat16), "gz", axis=0, tiled=True)
    return (input_grad, first.astype(jnp.bfloat16), second.astype(jnp.bfloat16), down_grad)


def solution(mesh):
    in_specs = (
        P("gy", "gx"),
        P("gy", "gx"),
        P("gx", ("gy", "gz")),
        P("gx", ("gy", "gz")),
        P("gx", ("gy", "gz")),
        P("gx", ("gy", "gz")),
        P(("gy", "gz"), "gx"),
    )
    out_specs = (P("gy", "gx"), P("gx", ("gy", "gz")), P("gx", ("gy", "gz")), P(("gy", "gz"), "gx"))
    return jax.shard_map(shards, mesh=mesh, in_specs=in_specs, out_specs=out_specs, check_vma=False)
```

profile of v0, /device:TPU:0, one launch (start us, length us, event | category | flops | bytes accessed | tf_op | source)
XLA Modules:
  0.0 951.3 jit_solution(15693381875679629747)
XLA Ops:
  7.2 0.0 all-gather.6.cloned.1.call-start
  7.2 0.7 all-gather.6.cloned.1.call-update
  7.9 0.0 all-gather.10.cloned.1.call-start
  7.9 0.7 all-gather.10.cloned.1.call-update
  8.6 0.0 all-gather.8.cloned.1.call-start
  8.7 0.7 all-gather.8.cloned.1.call-update
  9.4 0.0 all-reduce.2.cloned.1.call-start
  9.4 37.3 %all-gather.6.cloned.1.call-done = bf16[1024,2048]{1,0:T(8,128)(2,1)} async-done(((bf16[256,2048]{1,0:T(8,128)(2,1)}), bf16[1024,2048]{1,0:T(8,128)(2,1)}) %all-gather.6.cloned.1.call-update) | async-done | bytes 4194320 | tf_op jit(solution)/shard_map/all_gather | solution.py:36
  46.8 22.5 %fusion.17 = f32[1024,3328]{1,0:T(8,128)} fusion(bf16[1024,2048]{1,0:T(8,128)(2,1)} %all-gather.6.cloned.1.call-done, bf16[3328,2048]{1,0:T(8,128)(2,1)} %param.13), kind=kOutput, calls=%fused_computation.24 | convolution fusion | flops 13958643712 | bytes 31457280 | tf_op jit(solution)/shard_map/dot_general | solution.py:41
  69.3 0.0 all-reduce.2.cloned.1.call-update
  69.3 0.0 all-gather.14.cloned.1.call-start
  69.4 0.5 all-gather.14.cloned.1.call-update
  69.9 0.2 reduce-scatter.2.cloned.1.call-start
  70.2 102.1 %all-gather.10.cloned.1.call-done = bf16[1024,3328]{1,0:T(8,128)(2,1)} async-done(((bf16[256,3328]{1,0:T(8,128)(2,1)}), bf16[1024,3328]{1,0:T(8,128)(2,1)}) %all-gather.10.cloned.1.call-update) | async-done | bytes 6815760 | tf_op jit(solution)/shard_map/all_gather | solution.py:38
  172.3 123.8 %all-gather.8.cloned.1.call-done = bf16[1024,3328]{1,0:T(8,128)(2,1)} async-done(((bf16[256,3328]{1,0:T(8,128)(2,1)}), bf16[1024,3328]{1,0:T(8,128)(2,1)}) %all-gather.8.cloned.1.call-update) | async-done | bytes 6815760 | tf_op jit(solution)/shard_map/all_gather | solution.py:39
  296.1 461.1 %all-reduce.2.cloned.1.call-done = f32[1024,3328]{1,0:T(8,128)} async-done(((f32[1024,3328]{1,0:T(8,128)}), f32[1024,3328]{1,0:T(8,128)}) %all-reduce.2.cloned.1.call-update) | async-done | bytes 13631504 | tf_op jit(solution)/shard_map/psum | solution.py:44
  757.1 12.2 %fusion.2 = bf16[1024,3328]{1,0:T(8,128)(2,1)S(1)} fusion(f32[1024,3328]{1,0:T(8,128)} %all-reduce.2.cloned.1.call-done, bf16[1024,3328]{1,0:T(8,128)(2,1)} %all-gather.8.cloned.1.call-done, bf16[1024,3328]{1,0:T(8,128)(2,1)} %all-gather.10.cloned.1.call-done), kind=kLoop, calls=%fused_computation.11 | loop fusion | flops 40894464 | bytes 34078720 | tf_op jit(solution)/shard_map/convert_element_type | solution.py:15
  769.3 0.0 copy-start
  769.3 2.9 copy-done
  772.2 18.1 %fusion.18 = f32[1024,2048]{1,0:T(8,128)} fusion(bf16[1024,3328]{1,0:T(8,128)(2,1)S(1)} %fusion.2, bf16[2048,3328]{1,0:T(8,128)(2,1)} %param.11), kind=kOutput, calls=%fused_computation.25 | convolution fusion | flops 13958643712 | bytes 28835840 | tf_op jit(solution)/shard_map/dot_general | solution.py:25
  790.3 24.1 %convolution_add_fusion = f32[1024,2048]{1,0:T(8,128)} fusion(f32[1024,2048]{1,0:T(8,128)} %fusion.18, bf16[2048,3328]{1,0:T(8,128)(2,1)} %param.12, f32[1024,3328]{1,0:T(8,128)} %all-reduce.2.cloned.1.call-done, bf16[1024,3328]{1,0:T(8,128)(2,1)} %all-gather.10.cloned.1.call-done), kind=kOutput, calls=%fused_computation.22 | convolution fusion | flops 13984595968 | bytes 50855936 | tf_op jit(solution)/shard_map/dot_general | solution.py:28
  814.4 0.0 reduce-scatter.2.cloned.1.call-update
  814.4 0.3 all-gather.12.cloned.1.call-start
  814.7 23.9 %convolution_convert_fusion = bf16[3328,2048]{1,0:T(8,128)(2,1)} fusion(bf16[1024,2048]{1,0:T(8,128)(2,1)} %all-gather.6.cloned.1.call-done, bf16[1024,3328]{1,0:T(8,128)(2,1)} %all-gather.8.cloned.1.call-done, bf16[1024,3328]{1,0:T(8,128)(2,1)} %all-gather.10.cloned.1.call-done), kind=kOutput, calls=%fused_computation.6 | convolution fusion | flops 13992722432 | bytes 31457280 | tf_op jit(solution)/shard_map/dot_general | solution.py:46
  838.6 0.0 all-gather.14.cloned.1.call-done
  838.6 23.5 %fusion.11 = bf16[2048,3328]{0,1:T(8,128)(2,1)} fusion(bf16[1024,2048]{1,0:T(8,128)(2,1)} %all-gather.14.cloned.1.call-done, f32[1024,3328]{1,0:T(8,128)} %all-reduce.2.cloned.1.call-done, bf16[1024,3328]{1,0:T(8,128)(2,1)} %all-gather.10.cloned.1.call-done), kind=kOutput, calls=%fused_computation.20 | convolution fusion | flops 13989314560 | bytes 38273024 | tf_op jit(solution)/shard_map/dot_general | solution.py:51
  862.1 22.0 %reduce-scatter.2.cloned.1.call-done = f32[128,2048]{1,0:T(8,128)} async-done(((f32[1024,2048]{1,0:T(8,128)}), f32[128,2048]{1,0:T(8,128)}) %reduce-scatter.2.cloned.1.call-update) | async-done | bytes 1048592 | tf_op jit(solution)/shard_map/reduce_scatter | solution.py:55
  884.1 2.1 convert_element_type.37
  886.2 0.0 all-gather.12.cloned.1.call-update
  886.2 21.0 %fusion.10 = bf16[2048,3328]{0,1:T(8,128)(2,1)} fusion(bf16[1024,3328]{1,0:T(8,128)(2,1)} %copy-done, bf16[1024,2048]{1,0:T(8,128)(2,1)} %all-gather.14.cloned.1.call-done), kind=kOutput, calls=%fused_computation.19 | convolution fusion | flops 13965459456 | bytes 24641536 | tf_op jit(solution)/shard_map/dot_general | solution.py:50
  907.3 17.4 %copy.11 = bf16[2048,3328]{1,0:T(8,128)(2,1)} copy(bf16[2048,3328]{0,1:T(8,128)(2,1)} %fusion.10) | data formatting | bytes 27262976
  924.7 17.4 %copy.12 = bf16[2048,3328]{1,0:T(8,128)(2,1)} copy(bf16[2048,3328]{0,1:T(8,128)(2,1)} %fusion.11) | data formatting | bytes 27262976
  942.1 0.0 all-gather.12.cloned.1.call-done
  942.2 2.3 copy.15
Async XLA Ops:
  7.2 39.6 %all-gather.6.cloned.1.call-start = ((), (), s32[]{:S(2)}) async-start(), calls=%async_computation.1 | async-start | bytes 5242880 | tf_op jit(solution)/shard_map/all_gather | solution.py:36
  7.9 164.4 %all-gather.10.cloned.1.call-start = ((), (), s32[]{:S(2)}) async-start(), calls=%async_computation.4 | async-start | bytes 8519680 | tf_op jit(solution)/shard_map/all_gather | solution.py:38
  8.6 287.4 %all-gather.8.cloned.1.call-start = ((), (), s32[]{:S(2)}) async-start(), calls=%async_computation.3 | async-start | bytes 8519680 | tf_op jit(solution)/shard_map/all_gather | solution.py:39
  9.4 747.8 %all-reduce.2.cloned.1.call-start = ((), (), s32[]{:S(2)}) async-start(), calls=%async_computation.2 | async-start | bytes 27262976 | tf_op jit(solution)/shard_map/psum | solution.py:44
  69.3 769.3 %all-gather.14.cloned.1.call-start = ((), (), s32[]{:S(2)}) async-start(), calls=%async_computation.7 | async-start | bytes 5242880 | tf_op jit(solution)/shard_map/all_gather | solution.py:49
  69.9 814.2 %reduce-scatter.2.cloned.1.call-start = ((), (), s32[]{:S(2)}) async-start(), calls=%async_computation.5 | async-start | bytes 9437184 | tf_op jit(solution)/shard_map/reduce_scatter | solution.py:55
  769.3 2.9 copy-start
  814.4 127.7 %all-gather.12.cloned.1.call-start = ((), (), s32[]{:S(2)}) async-start(), calls=%async_computation.6 | async-start | bytes 1572864 | tf_op jit(solution)/shard_map/all_gather | solution.py:61
Sparse Core Ops, SparseCore 0:
  9.6 37.1 all-gather.5
  48.3 123.9 all-gather.9
  173.9 122.1 all-gather.7
  299.0 458.1 all-reduce.1
  758.6 33.3 all-gather.13
  814.6 69.5 reduce-scatter.1
  886.4 21.2 all-gather.11
where the time goes:
time: 952 us; the launch traced here: 951 us
  waiting for transfers between devices  749 us (79%)
  matrix products  133 us (14%)
  local copies, waits for them, and re-layouts  40.1 us (4%)
  other arithmetic  14.3 us (2%)
  between operations  14.1 us (1%)
    psum x1, waiting for transfers between devices, shards(): grad_hidden = lax.psum(local_sum, 'gx')  461 us
    all_gather x1, waiting for transfers between devices, shards(): lax.all_gather(up_pre, 'gx', axis=0, tiled=True)  124 us
    all_gather x1, waiting for transfers between devices, shards(): lax.all_gather(gate_pre, 'gx', axis=0, tiled=True)  102 us
    unnamed x5, local copies, waits for them, and re-layouts  40.1 us
    all_gather x1, waiting for transfers between devices, shards(): cotangent_all = lax.all_gather(cotangent, 'gy', axis=0, tiled=True)  37.3 us
    dot_general x1, matrix products, compute(): lax.dot_general(grad_up, up_weight, over_cols, preferred_element_type=jnp...  24.1 us
    dot_general x1, matrix products, shards(): lax.dot_general(hidden, cotangent_all, over_rows, preferred_element_type=...  23.9 us
    dot_general x1, matrix products, shards(): lax.dot_general(segment, grad_up, over_rows, preferred_element_type=jnp.f...  23.5 us
  transfers between devices with their start and end apart: 7, of which 5 were waited for; matrix products, arithmetic and copies ran while one was open for 19% of the time, Pallas kernels for 0%

commit v1 on v0

--- a/solution.py
+++ b/solution.py
@@ -33,7 +33,12 @@
 
 
 def shards(activations, cotangent, gate_pre, up_pre, gate_weight, up_weight, down_weight):
-    cotangent_all = lax.all_gather(cotangent, "gy", axis=0, tiled=True)
+    ring = [cotangent]
+    for hop in range(3):
+        ring.append(lax.ppermute(ring[-1], "gy", [(dev, (dev + 1) % 4) for dev in range(4)]))
+    cotangent_all = jnp.roll(
+        jnp.concatenate(ring[::-1], axis=0), (lax.axis_index("gy") + 1) * ring[0].shape[0], axis=0
+    )
     gate_all, up_all = (
         lax.all_gather(gate_pre, "gx", axis=0, tiled=True),
         lax.all_gather(up_pre, "gx", axis=0, tiled=True),

time: 952 us -> 922 us (0.968)
  waiting for transfers between devices: 749 us -> 701 us
  local copies, waits for them, and re-layouts: 40.1 us -> 50.8 us
    all_gather x1, waiting for transfers between devices: 102 us -> 49.4 us  [shards(): lax.all_gather(gate_pre, 'gx', axis=0, tiled=True)]
    ppermute x0 -> x3, waiting for transfers between devices: none -> 43.1 us  [shards(): lax.ppermute(ring[-1], 'gy', [(dev, (dev + 1) % 4) for dev in range(4)])]
    all_gather x1 -> x0, waiting for transfers between devices: 37.3 us -> none  [shards(): cotangent_all = lax.all_gather(cotangent, 'gy', axis=0, tiled=True)]
    unnamed x5 -> x14, local copies, waits for them, and re-layouts: 40.1 us -> 49.8 us
  transfers between devices with their start and end apart: 7 -> 9, of which waited for: 5 -> 7; matrix products, arithmetic and copies ran while one was open for 19% -> 21% of each run, Pallas kernels for 0% -> 0%
where the time goes in v1:
time: 922 us; the launch traced here: 915 us
  waiting for transfers between devices  701 us (76%)
  matrix products  133 us (14%)
  local copies, waits for them, and re-layouts  50.8 us (6%)
  between operations  14.4 us (2%)
  other arithmetic  14.2 us (2%)
    psum x1, waiting for transfers between devices, shards(): grad_hidden = lax.psum(local_sum, 'gx')  461 us
    all_gather x1, waiting for transfers between devices, shards(): lax.all_gather(up_pre, 'gx', axis=0, tiled=True)  124 us
    unnamed x14, local copies, waits for them, and re-layouts  49.8 us
    all_gather x1, waiting for transfers between devices, shards(): lax.all_gather(gate_pre, 'gx', axis=0, tiled=True)  49.4 us
    ppermute x3, waiting for transfers between devices, shards(): lax.ppermute(ring[-1], 'gy', [(dev, (dev + 1) % 4) for dev in range(4)])  43.1 us
    dot_general x1, matrix products, compute(): lax.dot_general(grad_up, up_weight, over_cols, preferred_element_type=jnp...  24.1 us
    dot_general x1, matrix products, shards(): lax.dot_general(hidden, cotangent_all, over_rows, preferred_element_type=...  24 us
    dot_general x1, matrix products, shards(): lax.dot_general(segment, grad_up, over_rows, preferred_element_type=jnp.f...  23.5 us
  transfers between devices with their start and end apart: 9, of which 7 were waited for; matrix products, arithmetic and copies ran while one was open for 21% of the time, Pallas kernels for 0%

profile of v1, /device:TPU:0, one launch (start us, length us, event | category | flops | bytes accessed | tf_op | source)
XLA Modules:
  0.0 915.5 jit_solution(8238232602193486680)
XLA Ops:
  7.2 0.0 copy-start.1
  7.2 0.0 all-gather.7.cloned.1.call-start
  7.2 0.7 all-gather.7.cloned.1.call-update
  7.9 0.0 all-gather.5.cloned.1.call-start
  8.0 0.7 all-gather.5.cloned.1.call-update
  8.7 0.0 all-reduce.2.cloned.1.call-start
  8.7 0.5 collective-permute-start
  9.2 14.6 %collective-permute-done = bf16[256,2048]{1,0:T(8,128)(2,1)S(1)} collective-permute-done((bf16[256,2048]{1,0:T(8,128)(2,1)}, bf16[256,2048]{1,0:T(8,128)(2,1)S(1)}, u32[]{:S(2)}, u32[]{:S(2)}) %collective-permute-start) | collective-permute-done | bytes 1048608 | tf_op jit(solution)/shard_map/ppermute | solution.py:38
  23.8 0.0 collective-permute-start.1
  23.9 14.2 %collective-permute-done.1 = bf16[256,2048]{1,0:T(8,128)(2,1)S(1)} collective-permute-done((bf16[256,2048]{1,0:T(8,128)(2,1)S(1)}, bf16[256,2048]{1,0:T(8,128)(2,1)S(1)}, u32[]{:S(2)}, u32[]{:S(2)}) %collective-permute-start.1) | collective-permute-done | bytes 1048608 | tf_op jit(solution)/shard_map/ppermute | solution.py:38
  38.1 0.0 collective-permute-start.2
  38.1 14.3 %collective-permute-done.2 = bf16[256,2048]{1,0:T(8,128)(2,1)} collective-permute-done((bf16[256,2048]{1,0:T(8,128)(2,1)S(1)}, bf16[256,2048]{1,0:T(8,128)(2,1)}, u32[]{:S(2)}, u32[]{:S(2)}) %collective-permute-start.2) | collective-permute-done | bytes 1048608 | tf_op jit(solution)/shard_map/ppermute | solution.py:38
  52.4 2.3 constant_dynamic-update-slice_fusion.7
  54.7 1.0 constant_dynamic-update-slice_fusion.6
  55.7 1.0 constant_dynamic-update-slice_fusion.5
  56.8 0.0 copy-done.1
  56.8 1.0 constant_dynamic-update-slice_fusion.4
  57.8 2.3 constant_dynamic-update-slice_fusion.3
  60.1 1.0 constant_dynamic-update-slice_fusion.2
  61.2 1.0 constant_dynamic-update-slice_fusion.1
  62.2 1.0 constant_dynamic-update-slice_fusion
  63.2 22.6 %fusion.15 = f32[1024,3328]{1,0:T(8,128)} fusion(bf16[3328,2048]{1,0:T(8,128)(2,1)} %param.13, bf16[2048,2048]{1,0:T(8,128)(2,1)} %constant_dynamic-update-slice_fusion, s32[]{:T(128)S(6)} %select_n.14), kind=kOutput, calls=%fused_computation.24 | convolution fusion | flops 13958643712 | bytes 31457284 | tf_op jit(solution)/shard_map/dot_general | solution.py:46
  85.9 0.0 all-reduce.2.cloned.1.call-update
  85.9 0.0 all-gather.11.cloned.1.call-start
  85.9 0.5 all-gather.11.cloned.1.call-update
  86.5 0.3 reduce-scatter.2.cloned.1.call-start
  86.8 49.4 %all-gather.7.cloned.1.call-done = bf16[1024,3328]{1,0:T(8,128)(2,1)} async-done(((bf16[256,3328]{1,0:T(8,128)(2,1)}), bf16[1024,3328]{1,0:T(8,128)(2,1)}) %all-gather.7.cloned.1.call-update) | async-done | bytes 6815760 | tf_op jit(solution)/shard_map/all_gather | solution.py:43
  136.2 123.8 %all-gather.5.cloned.1.call-done = bf16[1024,3328]{1,0:T(8,128)(2,1)} async-done(((bf16[256,3328]{1,0:T(8,128)(2,1)}), bf16[1024,3328]{1,0:T(8,128)(2,1)}) %all-gather.5.cloned.1.call-update) | async-done | bytes 6815760 | tf_op jit(solution)/shard_map/all_gather | solution.py:44
  260.0 461.2 %all-reduce.2.cloned.1.call-done = f32[1024,3328]{1,0:T(8,128)} async-done(((f32[1024,3328]{1,0:T(8,128)}), f32[1024,3328]{1,0:T(8,128)}) %all-reduce.2.cloned.1.call-update) | async-done | bytes 13631504 | tf_op jit(solution)/shard_map/psum | solution.py:49
  721.2 12.2 %fusion.2 = bf16[1024,3328]{1,0:T(8,128)(2,1)S(1)} fusion(f32[1024,3328]{1,0:T(8,128)} %all-reduce.2.cloned.1.call-done, bf16[1024,3328]{1,0:T(8,128)(2,1)} %all-gather.5.cloned.1.call-done, bf16[1024,3328]{1,0:T(8,128)(2,1)} %all-gather.7.cloned.1.call-done), kind=kLoop, calls=%fused_computation.11 | loop fusion | flops 40894464 | bytes 34078720 | tf_op jit(solution)/shard_map/convert_element_type | solution.py:15
  733.4 0.0 copy-start
  733.4 2.8 copy-done
  736.2 18.1 %fusion.22 = f32[1024,2048]{1,0:T(8,128)} fusion(bf16[1024,3328]{1,0:T(8,128)(2,1)S(1)} %fusion.2, bf16[2048,3328]{1,0:T(8,128)(2,1)} %param.11), kind=kOutput, calls=%fused_computation.37 | convolution fusion | flops 13958643712 | bytes 28835840 | tf_op jit(solution)/shard_map/dot_general | solution.py:25
  754.3 24.1 %convolution_add_fusion = f32[1024,2048]{1,0:T(8,128)} fusion(f32[1024,2048]{1,0:T(8,128)} %fusion.22, bf16[2048,3328]{1,0:T(8,128)(2,1)} %param.12, f32[1024,3328]{1,0:T(8,128)} %all-reduce.2.cloned.1.call-done, bf16[1024,3328]{1,0:T(8,128)(2,1)} %all-gather.7.cloned.1.call-done), kind=kOutput, calls=%fused_computation.22 | convolution fusion | flops 13984595968 | bytes 50855936 | tf_op jit(solution)/shard_map/dot_general | solution.py:28
  778.4 0.0 reduce-scatter.2.cloned.1.call-update
  778.5 0.6 all-gather.9.cloned.1.call-start
  779.0 24.0 %convolution_convert_fusion = bf16[3328,2048]{1,0:T(8,128)(2,1)} fusion(bf16[1024,3328]{1,0:T(8,128)(2,1)} %all-gather.5.cloned.1.call-done, bf16[1024,3328]{1,0:T(8,128)(2,1)} %all-gather.7.cloned.1.call-done, bf16[2048,2048]{1,0:T(8,128)(2,1)} %constant_dynamic-update-slice_fusion, s32[]{:T(128)S(6)} %select_n.14), kind=kOutput, calls=%fused_computation.6 | convolution fusion | flops 13992722432 | bytes 31457284 | tf_op jit(solution)/shard_map/dot_general | solution.py:51
  803.0 0.0 all-gather.11.cloned.1.call-done
  803.0 23.5 %fusion.11 = bf16[2048,3328]{0,1:T(8,128)(2,1)} fusion(bf16[1024,2048]{1,0:T(8,128)(2,1)} %all-gather.11.cloned.1.call-done, f32[1024,3328]{1,0:T(8,128)} %all-reduce.2.cloned.1.call-done, bf16[1024,3328]{1,0:T(8,128)(2,1)} %all-gather.7.cloned.1.call-done), kind=kOutput, calls=%fused_computation.20 | convolution fusion | flops 13989314560 | bytes 38273024 | tf_op jit(solution)/shard_map/dot_general | solution.py:56
  826.5 21.7 %reduce-scatter.2.cloned.1.call-done = f32[128,2048]{1,0:T(8,128)} async-done(((f32[1024,2048]{1,0:T(8,128)}), f32[128,2048]{1,0:T(8,128)}) %reduce-scatter.2.cloned.1.call-update) | async-done | bytes 1048592 | tf_op jit(solution)/shard_map/reduce_scatter | solution.py:60
  848.2 2.1 convert_element_type.37
  850.2 0.0 all-gather.9.cloned.1.call-update
  850.3 20.9 %fusion.10 = bf16[2048,3328]{0,1:T(8,128)(2,1)} fusion(bf16[1024,3328]{1,0:T(8,128)(2,1)} %copy-done, bf16[1024,2048]{1,0:T(8,128)(2,1)} %all-gather.11.cloned.1.call-done), kind=kOutput, calls=%fused_computation.19 | convolution fusion | flops 13965459456 | bytes 24641536 | tf_op jit(solution)/shard_map/dot_general | solution.py:55
  871.2 17.4 %copy.12 = bf16[2048,3328]{1,0:T(8,128)(2,1)} copy(bf16[2048,3328]{0,1:T(8,128)(2,1)} %fusion.11) | data formatting | bytes 27262976
  888.6 17.4 %copy.11 = bf16[2048,3328]{1,0:T(8,128)(2,1)} copy(bf16[2048,3328]{0,1:T(8,128)(2,1)} %fusion.10) | data formatting | bytes 27262976
  906.1 0.0 all-gather.9.cloned.1.call-done
  906.1 2.3 copy.22
Async XLA Ops:
  7.2 49.6 %copy-start.1 = (bf16[256,2048]{1,0:T(8,128)(2,1)S(1)}, bf16[256,2048]{1,0:T(8,128)(2,1)}, u32[]{:S(2)}) copy-start(bf16[256,2048]{1,0:T(8,128)(2,1)} %param.8) | copy-start | bytes 3145732
  7.2 129.1 %all-gather.7.cloned.1.call-start = ((), (), s32[]{:S(2)}) async-start(), calls=%async_computation.3 | async-start | bytes 8519680 | tf_op jit(solution)/shard_map/all_gather | solution.py:43
  7.9 252.1 %all-gather.5.cloned.1.call-start = ((), (), s32[]{:S(2)}) async-start(), calls=%async_computation.2 | async-start | bytes 8519680 | tf_op jit(solution)/shard_map/all_gather | solution.py:44
  8.7 712.6 %all-reduce.2.cloned.1.call-start = ((), (), s32[]{:S(2)}) async-start(), calls=%async_computation.1 | async-start | bytes 27262976 | tf_op jit(solution)/shard_map/psum | solution.py:49
  8.7 15.1 %collective-permute-start = (bf16[256,2048]{1,0:T(8,128)(2,1)}, bf16[256,2048]{1,0:T(8,128)(2,1)S(1)}, u32[]{:S(2)}, u32[]{:S(2)}) collective-permute-start(bf16[256,2048]{1,0:T(8,128)(2,1)} %param.8), channel_id=1, source_target_pairs={{0,2},{2,4},{4,6},{6,0},{1,3},{3,5},{5,7},{7,1},{8,10},{10,12},{12... | collective-permute-start | bytes 3145736 | tf_op jit(solution)/shard_map/ppermute | solution.py:38
  23.8 14.2 %collective-permute-start.1 = (bf16[256,2048]{1,0:T(8,128)(2,1)S(1)}, bf16[256,2048]{1,0:T(8,128)(2,1)S(1)}, u32[]{:S(2)}, u32[]{:S(2)}) collective-permute-start(bf16[256,2048]{1,0:T(8,128)(2,1)S(1)} %collective-permute-done), channel_id=1, source_target_pairs={{0,2},{2,4},{4,6},{6,0},{1,3},{3,5},{5,7},{7,1},{8,10},{10,12},{12... | collective-permute-start | bytes 3145736 | tf_op jit(solution)/shard_map/ppermute | solution.py:38
  38.1 14.3 %collective-permute-start.2 = (bf16[256,2048]{1,0:T(8,128)(2,1)S(1)}, bf16[256,2048]{1,0:T(8,128)(2,1)}, u32[]{:S(2)}, u32[]{:S(2)}) collective-permute-start(bf16[256,2048]{1,0:T(8,128)(2,1)S(1)} %collective-permute-done.1), channel_id=1, source_target_pairs={{0,2},{2,4},{4,6},{6,0},{1,3},{3,5},{5,7},{7,1},{8,10},{10,12},{12... | collective-permute-start | bytes 3145736 | tf_op jit(solution)/shard_map/ppermute | solution.py:38
  85.9 717.1 %all-gather.11.cloned.1.call-start = ((), (), s32[]{:S(2)}) async-start(), calls=%async_computation.6 | async-start | bytes 5242880 | tf_op jit(solution)/shard_map/all_gather | solution.py:54
  86.5 761.7 %reduce-scatter.2.cloned.1.call-start = ((), (), s32[]{:S(2)}) async-start(), calls=%async_computation.4 | async-start | bytes 9437184 | tf_op jit(solution)/shard_map/reduce_scatter | solution.py:60
  733.4 2.8 copy-start
  778.5 127.6 %all-gather.9.cloned.1.call-start = ((), (), s32[]{:S(2)}) async-start(), calls=%async_computation.5 | async-start | bytes 1572864 | tf_op jit(solution)/shard_map/all_gather | solution.py:66
Sparse Core Ops, SparseCore 0:
  9.6 126.6 all-gather.6
  137.8 122.1 all-gather.4
  263.1 458.1 all-reduce.1
  722.6 33.3 all-gather.10
  778.6 69.5 reduce-scatter.1
  850.4 21.2 all-gather.8
